TPU v7x, 128 devices: a whole 4x4x4 slice. The times are simulated.
128 devices in a mesh: fsdp: 8 (over y_lo, z), ctx: 4 (over y_hi, core), tp: 4 (over x).
Axes of the slice: x: 4, y: 4 (y_hi: 2, y_lo: 2; y = y_hi * 2 + y_lo), z: 4, core: 2. Of those that a mesh axis runs over, the one named last changes fastest.
Arguments:
- inputs: bfloat16 [32, 1024, 960], P(('fsdp', 'tp'), 'ctx'), may hold values from -6 to 6
- seq_live: int32 [32], P(('fsdp', 'tp')), may hold values from 0 to 1, as said below
- positions: int32 [32, 1024], P(('fsdp', 'tp'), 'ctx'), may hold values from 0 to 2046, as said below
- gain_attn: bfloat16 [960], P('fsdp'), may hold values from 0.5 to 1.5
- w_query: bfloat16 [960, 960], P('fsdp'), may hold values from -0.75 to 0.75
- w_key: bfloat16 [960, 320], P('fsdp'), may hold values from -0.75 to 0.75
- w_value: bfloat16 [960, 320], P('fsdp'), may hold values from -0.1875 to 0.1875
- w_out: bfloat16 [960, 960], P('fsdp'), may hold values from -1.5 to 1.5
- gain_mlp: bfloat16 [960], P('fsdp'), may hold values from 0.5 to 1.5
- w_gate: bfloat16 [960, 2560], P('fsdp', 'tp'), may hold values from -0.1875 to 0.1875
- w_up: bfloat16 [960, 2560], P('fsdp', 'tp'), may hold values from -0.1875 to 0.1875
- w_down: bfloat16 [960, 2560], P('fsdp', 'tp'), may hold values from -0.125 to 0.125
- cotangent: float32 [32, 1024, 960], P(('fsdp', 'tp'), 'ctx'), may hold values from -6 to 6
Outputs:
- layer_out: float32 [32, 1024, 960], P(('fsdp', 'tp'), 'ctx')
- dinputs: float32 [32, 1024, 960], P(('fsdp', 'tp'), 'ctx')
- dgain_attn: float32 [960], P('fsdp')
- dw_query: float32 [960, 960], P('fsdp')
- dw_key: float32 [960, 320], P('fsdp')
- dw_value: float32 [960, 320], P('fsdp')
- dw_out: float32 [960, 960], P('fsdp')
- dgain_mlp: float32 [960], P('fsdp')
- dw_gate: float32 [960, 2560], P('fsdp', 'tp')
- dw_up: float32 [960, 2560], P('fsdp', 'tp')
- dw_down: float32 [960, 2560], P('fsdp', 'tp')
Inputs may be any that keep to these rules, and one draw needn't show every extreme that they name: `seq_live`: the slots fall into equal blocks of consecutive slots, one block for each index of fsdp; each block holds either only 1s or exactly one 0, at any slot of the block, and both kinds of block occur. `positions`: each row starts at 0 and rises by 1 or 2 from token to token; the first slot's row rises by 2 throughout.
All inputs are finite; a program needn't handle non-finite values.
Results may differ from a plain program's by a relative error of at most 0.025.
Values may be sent and summed in bfloat16 or wider, within the bound.
No kernel may reach another device: no remote copies, remote signals or barrier semaphores. Data moves between devices by JAX's collectives and lax.ppermute only.
A program may use at most 128 MiB of HBM per device.

v0:
```python
import math
import jax
import jax.numpy as jnp
from jax import lax
from jax.sharding import PartitionSpec as P

QH = 15
KVH = 5
HEAD = 64
EPSILON = 1e-05
ROPE_BASE = 100000.0


def joined_along(tiles, dim):
    tiles = jnp.moveaxis(tiles, 0, dim)
    lengths = tiles.shape
    return tiles.reshape(*lengths[:dim], lengths[dim] * lengths[dim + 1], *lengths[dim + 2 :])


def from_everyone(shard, axis):
    copies = jnp.broadcast_to(shard, (lax.axis_size(axis), *shard.shape))
    return lax.all_to_all(copies, axis, split_axis=0, concat_axis=0, tiled=True)


def collect(shard, axis, dim):
    return joined_along(from_everyone(shard, axis), dim)


def cut_along(shard, dim, devices):
    lengths = shard.shape
    tiles = shard.reshape(*lengths[:dim], devices, lengths[dim] // devices, *lengths[dim + 1 :])
    return jnp.moveaxis(tiles, dim, 0)


def sent_and_summed(shard, axis, dim):
    tiles = cut_along(shard, dim, lax.axis_size(axis))
    arrived = lax.all_to_all(tiles, axis, split_axis=0, concat_axis=0, tiled=True)
    return arrived.astype(jnp.float32).sum(axis=0)


def sum_at_owner(shard, axis, dim):
    tiles = cut_along(shard, dim, lax.axis_size(axis))
    arrived = lax.all_to_all(tiles, axis, split_axis=0, concat_axis=0, tiled=True)
    return arrived.sum(axis=0)


def sent_together(arrays, axis, dim, along):
    columns = [a.reshape(*a.shape[:along], -1) for a in arrays]
    both = jnp.concatenate(columns, axis=along)
    out, at, done = (lax.psum_scatter(both, axis, scatter_dimension=dim, tiled=True), 0, [])
    for a, column in zip(arrays, columns):
        slab = out[..., at : at + column.shape[along]]
        done.append(slab.reshape(*slab.shape[:along], *a.shape[along:]))
        at += column.shape[along]
    return tuple(done)


def over_copies(shard, axis):
    return from_everyone(shard, axis).astype(jnp.float32).sum(axis=0)


def rope_tables(position_ids):
    half_dim = HEAD // 2
    freq_index = jnp.arange(half_dim, dtype=jnp.float32)
    inverse = jnp.exp(freq_index * (-2.0 * math.log(ROPE_BASE) / HEAD))
    angles = position_ids.astype(jnp.float32)[:, None] * inverse[None, :]
    return (jnp.cos(angles)[:, None, :], jnp.sin(angles)[:, None, :])


def rotate(tensor, cos_table, sin_table):
    half_dim = tensor.shape[-1] // 2
    first_half = tensor[..., :half_dim]
    second_half = tensor[..., half_dim:]
    return jnp.concatenate(
        [
            first_half * cos_table - second_half * sin_table,
            second_half * cos_table + first_half * sin_table,
        ],
        -1,
    )


def rotate_back(tensor, cos_table, sin_table):
    half_dim = tensor.shape[-1] // 2
    first_half = tensor[..., :half_dim]
    second_half = tensor[..., half_dim:]
    return jnp.concatenate(
        [
            first_half * cos_table + second_half * sin_table,
            second_half * cos_table - first_half * sin_table,
        ],
        -1,
    )


def rms_forward(stream, gain_vector):
    scale_inv = lax.rsqrt(jnp.mean(stream * stream, -1, keepdims=True) + EPSILON)
    normed = stream * scale_inv
    return (scale_inv, normed, (normed * gain_vector.astype(jnp.float32)).astype(jnp.bfloat16))


def rms_backward(upstream, scale_inv, normed, gain_vector):
    scaled = upstream * gain_vector.astype(jnp.float32)
    inner_mean = jnp.mean(scaled * normed, -1, keepdims=True)
    return (scale_inv * (scaled - normed * inner_mean), jnp.sum(upstream * normed, 0))


def masked_scores(head_queries, head_keys, allowed, score_scale):
    scores = (
        jnp.einsum("sqgd,skd->sgqk", head_queries, head_keys, preferred_element_type=jnp.float32)
        * score_scale
    )
    return jnp.where(allowed, scores, -1e30)


def shards(
    inputs,
    seq_live,
    positions,
    gain_attn,
    w_query,
    w_key,
    w_value,
    w_out,
    gain_mlp,
    w_gate,
    w_up,
    w_down,
    cotangent,
):
    (
        full_gain_attn,
        full_gain_mlp,
        full_query,
        full_key,
        full_value,
        full_out,
        full_gate,
        full_up,
        full_down,
    ) = (
        lax.all_gather(gain_attn, "fsdp", axis=0, tiled=True),
        lax.all_gather(gain_mlp, "fsdp", axis=0, tiled=True),
        lax.all_gather(w_query, "fsdp", axis=0, tiled=True),
        lax.all_gather(w_key, "fsdp", axis=0, tiled=True),
        lax.all_gather(w_value, "fsdp", axis=0, tiled=True),
        lax.all_gather(w_out, "fsdp", axis=0, tiled=True),
        lax.all_gather(w_gate, "fsdp", axis=0, tiled=True),
        lax.all_gather(w_up, "fsdp", axis=0, tiled=True),
        lax.all_gather(w_down, "fsdp", axis=0, tiled=True),
    )
    seq_dev, local_len, model_width = inputs.shape
    full_len = local_len * lax.axis_size("ctx")
    row_count = seq_dev * local_len
    group_size = QH // KVH
    kv_dim = KVH * HEAD
    score_scale = 1.0 / math.sqrt(HEAD)
    contract_rows = (((0,), (0,)), ((), ()))
    contract_cols = (((1,), (1,)), ((), ()))
    stream = inputs.astype(jnp.float32).reshape(row_count, model_width)
    inv_one, normed_one, hidden_one = rms_forward(stream, full_gain_attn)
    cos_table, sin_table = rope_tables(positions.reshape(row_count))
    query_lin = jnp.dot(hidden_one, full_query, preferred_element_type=jnp.float32).reshape(
        row_count, QH, HEAD
    )
    queries = rotate(query_lin, cos_table, sin_table).astype(jnp.bfloat16)
    key_lin = jnp.dot(hidden_one, full_key, preferred_element_type=jnp.float32).reshape(
        row_count, KVH, HEAD
    )
    key_rows = rotate(key_lin, cos_table, sin_table).astype(jnp.bfloat16)
    value_rows = jnp.dot(hidden_one, full_value, preferred_element_type=jnp.float32).astype(
        jnp.bfloat16
    )
    packed = jnp.concatenate([key_rows.reshape(row_count, kv_dim), value_rows], 1).reshape(
        seq_dev, local_len, 2 * kv_dim
    )
    gathered = collect(packed, "ctx", 1)
    all_keys = gathered[..., :kv_dim].reshape(seq_dev, full_len, KVH, HEAD)
    all_values = gathered[..., kv_dim:].reshape(seq_dev, full_len, KVH, HEAD)
    query_groups = queries.reshape(seq_dev, local_len, KVH, group_size, HEAD)
    query_index = lax.axis_index("ctx") * local_len + jnp.arange(local_len, dtype=jnp.int32)
    allowed = query_index[:, None] >= jnp.arange(full_len, dtype=jnp.int32)[None, :]
    log_totals = []
    attended_parts = []
    for head_index in range(KVH):
        scores = masked_scores(
            query_groups[:, :, head_index], all_keys[:, :, head_index], allowed, score_scale
        )
        row_top = jnp.max(scores, -1, keepdims=True)
        log_total = row_top + jnp.log(jnp.sum(jnp.exp(scores - row_top), -1, keepdims=True))
        probs_b = jnp.exp(scores - log_total).astype(jnp.bfloat16)
        attended_parts.append(
            jnp.einsum(
                "sgqk,skd->sqgd",
                probs_b,
                all_values[:, :, head_index],
                preferred_element_type=jnp.float32,
            )
        )
        log_totals.append(log_total)
    attended = jnp.stack(attended_parts, 2).astype(jnp.bfloat16).reshape(row_count, QH * HEAD)
    mid_stream = stream + jnp.dot(attended, full_out, preferred_element_type=jnp.float32)
    inv_two, normed_two, hidden_two = rms_forward(mid_stream, full_gain_mlp)
    mlp_input = collect(hidden_two.reshape(seq_dev, local_len, model_width), "tp", 0).reshape(
        -1, model_width
    )
    gate_pre = jnp.dot(mlp_input, full_gate, preferred_element_type=jnp.float32)
    up_pre = jnp.dot(mlp_input, full_up, preferred_element_type=jnp.float32)
    sigmoid_gate = jax.nn.sigmoid(gate_pre)
    activated = (gate_pre * sigmoid_gate * up_pre).astype(jnp.bfloat16)
    partial_out = lax.dot_general(
        activated, full_down, contract_cols, preferred_element_type=jnp.float32
    )
    mlp_out = sent_and_summed(
        partial_out.reshape(-1, local_len, model_width).astype(jnp.bfloat16), "tp", 0
    ).reshape(row_count, model_width)
    layer_out = mid_stream + mlp_out
    upstream = (cotangent * seq_live.astype(jnp.float32)[:, None, None]).reshape(
        row_count, model_width
    )
    upstream_b = upstream.astype(jnp.bfloat16)
    grad_rows = collect(upstream_b.reshape(seq_dev, local_len, model_width), "tp", 0).reshape(
        -1, model_width
    )
    grad_act = jnp.dot(grad_rows, full_down, preferred_element_type=jnp.float32)
    up_back = (grad_act * gate_pre * sigmoid_gate).astype(jnp.bfloat16)
    gate_back = (grad_act * up_pre * sigmoid_gate * (1.0 + gate_pre * (1.0 - sigmoid_gate))).astype(
        jnp.bfloat16
    )
    grad_down_full = lax.dot_general(
        grad_rows, activated, contract_rows, preferred_element_type=jnp.float32
    )
    grad_gate_full = lax.dot_general(
        mlp_input, gate_back, contract_rows, preferred_element_type=jnp.float32
    )
    grad_up_full = lax.dot_general(
        mlp_input, up_back, contract_rows, preferred_element_type=jnp.float32
    )
    partial_in = lax.dot_general(
        gate_back, full_gate, contract_cols, preferred_element_type=jnp.float32
    ) + lax.dot_general(up_back, full_up, contract_cols, preferred_element_type=jnp.float32)
    grad_hidden_two = sum_at_owner(partial_in.reshape(-1, local_len, model_width), "tp", 0).reshape(
        row_count, model_width
    )
    back_two, grad_gain_two = rms_backward(grad_hidden_two, inv_two, normed_two, full_gain_mlp)
    grad_mid = upstream + back_two
    grad_mid_b = grad_mid.astype(jnp.bfloat16)
    grad_out_full = lax.dot_general(
        attended, grad_mid_b, contract_rows, preferred_element_type=jnp.float32
    )
    grad_attended = lax.dot_general(
        grad_mid_b, full_out, contract_cols, preferred_element_type=jnp.float32
    ).astype(jnp.bfloat16)
    grad_attended = grad_attended.reshape(seq_dev, local_len, KVH, group_size, HEAD)
    key_grad_parts = []
    value_grad_parts = []
    query_grad_parts = []
    for head_index in range(KVH):
        head_queries = query_groups[:, :, head_index]
        head_keys = all_keys[:, :, head_index]
        head_values = all_values[:, :, head_index]
        head_grads = grad_attended[:, :, head_index]
        scores = masked_scores(head_queries, head_keys, allowed, score_scale)
        softmax = jnp.exp(scores - log_totals[head_index])
        probs_b = softmax.astype(jnp.bfloat16)
        grad_probs = jnp.einsum(
            "sqgd,skd->sgqk", head_grads, head_values, preferred_element_type=jnp.float32
        )
        row_inner = jnp.sum(softmax * grad_probs, -1, keepdims=True)
        grad_scores = (softmax * (grad_probs - row_inner) * score_scale).astype(jnp.bfloat16)
        value_grad_parts.append(
            jnp.einsum("sgqk,sqgd->skd", probs_b, head_grads, preferred_element_type=jnp.float32)
        )
        key_grad_parts.append(
            jnp.einsum(
                "sgqk,sqgd->skd", grad_scores, head_queries, preferred_element_type=jnp.float32
            )
        )
        query_grad_parts.append(
            jnp.einsum("sgqk,skd->sqgd", grad_scores, head_keys, preferred_element_type=jnp.float32)
        )
    grad_keys_all = jnp.stack(key_grad_parts, 2).reshape(seq_dev, full_len, kv_dim)
    grad_values_all = jnp.stack(value_grad_parts, 2).reshape(seq_dev, full_len, kv_dim)
    grad_queries = jnp.stack(query_grad_parts, 2).reshape(row_count, QH, HEAD)
    packed_grads = jnp.concatenate([grad_keys_all, grad_values_all], -1)
    own_grads = sum_at_owner(packed_grads, "ctx", 1).reshape(row_count, 2 * kv_dim)
    grad_key_lin = (
        rotate_back(own_grads[:, :kv_dim].reshape(row_count, KVH, HEAD), cos_table, sin_table)
        .astype(jnp.bfloat16)
        .reshape(row_count, kv_dim)
    )
    grad_value_lin = own_grads[:, kv_dim:].astype(jnp.bfloat16)
    grad_query_lin = (
        rotate_back(grad_queries, cos_table, sin_table)
        .astype(jnp.bfloat16)
        .reshape(row_count, QH * HEAD)
    )
    grad_query_full = lax.dot_general(
        hidden_one, grad_query_lin, contract_rows, preferred_element_type=jnp.float32
    )
    grad_key_full = lax.dot_general(
        hidden_one, grad_key_lin, contract_rows, preferred_element_type=jnp.float32
    )
    grad_value_full = lax.dot_general(
        hidden_one, grad_value_lin, contract_rows, preferred_element_type=jnp.float32
    )
    grad_hidden_one = lax.dot_general(
        grad_query_lin, full_query, contract_cols, preferred_element_type=jnp.float32
    )
    grad_hidden_one = grad_hidden_one + lax.dot_general(
        grad_key_lin, full_key, contract_cols, preferred_element_type=jnp.float32
    )
    grad_hidden_one = grad_hidden_one + lax.dot_general(
        grad_value_lin, full_value, contract_cols, preferred_element_type=jnp.float32
    )
    back_one, grad_gain_one = rms_backward(grad_hidden_one, inv_one, normed_one, full_gain_attn)
    grad_input = grad_mid + back_one
    (
        share_gain_one,
        share_gain_two,
        share_query,
        share_key,
        share_value,
        share_out,
        share_gate,
        share_up,
        share_down,
    ) = (
        lax.psum_scatter(
            grad_gain_one.astype(jnp.bfloat16), "fsdp", scatter_dimension=0, tiled=True
        ).astype(jnp.float32),
        *tuple(
            (
                part.astype(jnp.float32)
                for part in sent_together(
                    (
                        grad_gain_two.astype(jnp.bfloat16),
                        grad_query_full.astype(jnp.bfloat16),
                        grad_key_full.astype(jnp.bfloat16),
                        grad_value_full.astype(jnp.bfloat16),
                        grad_out_full.astype(jnp.bfloat16),
                        grad_gate_full.astype(jnp.bfloat16),
                        grad_up_full.astype(jnp.bfloat16),
                        grad_down_full.astype(jnp.bfloat16),
                    ),
                    "fsdp",
                    0,
                    1,
                )
            )
        ),
    )
    share_gate, share_up, share_down = (
        over_copies(share_gate.astype(jnp.bfloat16), "ctx").astype(jnp.float32),
        over_copies(share_up.astype(jnp.bfloat16), "ctx").astype(jnp.float32),
        over_copies(share_down.astype(jnp.bfloat16), "ctx").astype(jnp.float32),
    )
    share_gain_one, share_gain_two, share_query, share_key, share_value, share_out = (
        lax.psum(share_gain_one.astype(jnp.bfloat16), ("ctx", "tp")).astype(jnp.float32),
        lax.psum(share_gain_two.astype(jnp.bfloat16), ("ctx", "tp")).astype(jnp.float32),
        lax.psum(share_query.astype(jnp.bfloat16), ("ctx", "tp")).astype(jnp.float32),
        lax.psum(share_key.astype(jnp.bfloat16), ("ctx", "tp")).astype(jnp.float32),
        lax.psum(share_value.astype(jnp.bfloat16), ("ctx", "tp")).astype(jnp.float32),
        lax.psum(share_out.astype(jnp.bfloat16), ("ctx", "tp")).astype(jnp.float32),
    )
    return (
        layer_out.reshape(seq_dev, local_len, model_width),
        grad_input.reshape(seq_dev, local_len, model_width),
        share_gain_one,
        share_query,
        share_key,
        share_value,
        share_out,
        share_gain_two,
        share_gate,
        share_up,
        share_down,
    )


def solution(mesh):
    placed = (
        P(("fsdp", "tp"), "ctx", None),
        P(("fsdp", "tp")),
        P(("fsdp", "tp"), "ctx"),
        P("fsdp"),
        P("fsdp", None),
        P("fsdp", None),
        P("fsdp", None),
        P("fsdp", None),
        P("fsdp"),
        P("fsdp", "tp"),
        P("fsdp", "tp"),
        P("fsdp", "tp"),
        P(("fsdp", "tp"), "ctx", None),
    )
    return jax.shard_map(
        shards,
        mesh=mesh,
        in_specs=placed,
        out_specs=(
            P(("fsdp", "tp"), "ctx", None),
            P(("fsdp", "tp"), "ctx", None),
            P("fsdp"),
            P("fsdp", None),
            P("fsdp", None),
            P("fsdp", None),
            P("fsdp", None),
            P("fsdp"),
            P("fsdp", "tp"),
            P("fsdp", "tp"),
            P("fsdp", "tp"),
        ),
        check_vma=False,
    )
```

profile of v0, /device:TPU:0, one launch (start us, length us, event | category | flops | bytes accessed | tf_op | source)
XLA Modules:
  0.0 709.2 jit_solution(10042288850751372710)
XLA Ops:
  9.4 31.9 %all-gather = bf16[8,120,320]{1,2,0:T(8,128)(2,1)S(1)} all-gather(bf16[1,120,320]{1,2,0:T(8,128)(2,1)} %bitcast.612), channel_id=1, replica_groups=mesh['fsdp'=8,'ctx'=4,'tp'=4] {'fsdp'}, dimensions={0}, use_global_device_ids=true | all-gather | bytes 691200 | tf_op jit(solution)/shard_map/all_gather | solution.py:145
  41.3 31.0 %all-gather.1 = bf16[8,120,320]{1,2,0:T(8,128)(2,1)S(1)} all-gather(bf16[1,120,320]{1,2,0:T(8,128)(2,1)} %bitcast.613), channel_id=1, replica_groups=mesh['fsdp'=8,'ctx'=4,'tp'=4] {'fsdp'}, dimensions={0}, use_global_device_ids=true | all-gather | bytes 691200 | tf_op jit(solution)/shard_map/all_gather | solution.py:146
  76.7 18.3 %all-reduce.5 = (bf16[960]{0:T(1024)(128)(2,1)S(1)}, bf16[960]{0:T(1024)(128)(2,1)S(1)}) all-reduce(bf16[960]{0:T(1024)(128)(2,1)S(1)} %dynamic-update-slice, bf16[960]{0:T(1024)(128)(2,1)S(1)} %dynamic-update-slice.1), channel_id=1, replica_groups=mesh['fsdp'=8,'ctx'=4,'tp'=4] {'fsdp'}, use_global_device_ids=true, to_apply=%add | all-reduce | flops 1920 | bytes 7680
  106.5 25.6 %all-to-all-done = bf16[4,1,256,640]{2,3,1,0:T(8,128)(2,1)S(1)} async-done(((bf16[4,1,256,640]{2,3,1,0:T(8,128)(2,1)}), bf16[4,1,256,640]{2,3,1,0:T(8,128)(2,1)S(1)}, u32[]{:S(2)}, u32[]{:S(2)}) %all-to-all-start) | async-done | bytes 1310752 | tf_op jit(solution)/shard_map/all_to_all | solution.py:22
  134.6 5.3 all-to-all-start.3
  170.0 4.8 all-to-all-start.1
  180.2 18.0 %all-to-all-done.1 = bf16[4,1,256,960]{2,3,1,0:T(8,128)(2,1)} async-done(((bf16[4,1,256,960]{2,3,1,0:T(8,128)(2,1)}), bf16[4,1,256,960]{2,3,1,0:T(8,128)(2,1)}, u32[]{:S(2)}, u32[]{:S(2)}) %all-to-all-start.1) | async-done | bytes 1966112 | tf_op jit(solution)/shard_map/all_to_all | solution.py:22
  203.0 5.3 fusion.133
  208.3 5.2 fusion.132
  213.5 6.0 all-gather.16.cloned.1.call-done
  219.6 7.8 %multiply_convert_fusion = (bf16[1024,640]{1,0:T(8,128)(2,1)}, bf16[1024,640]{1,0:T(8,128)(2,1)}, bf16[1024,640]{1,0:T(8,128)(2,1)S(1)}) fusion(f32[1024,640]{1,0:T(8,128)} %fusion.132, f32[1024,640]{1,0:T(8,128)} %fusion.133, bf16[1024,960]{0,1:T(8,128)(2,1)} %bitcast.598, bf16[960,640]{1,0:T(8,128)(2,1)} %all-gather.16.cloned.1.call-done), kind=kOutput, calls=%fused_computation.47 | convolution fusion | flops 1268776960 | bytes 12369920 | tf_op jit(solution)/shard_map/dot_general | solution.py:225
  250.9 5.4 reshape_reshape.11
  256.3 4.7 copy.201
  264.0 5.0 all-to-all-start.4
  269.0 4.8 convolution_convert_fusion.3
  282.2 26.7 %all-to-all-done.4 = f32[4,1,256,960]{2,3,1,0:T(8,128)} async-done(((f32[4,1,256,960]{2,3,1,0:T(8,128)}), f32[4,1,256,960]{2,3,1,0:T(8,128)}, u32[]{:S(2)}, u32[]{:S(2)}) %all-to-all-start.4) | async-done | bytes 3932192 | tf_op jit(solution)/shard_map/all_to_all | solution.py:43
  387.5 18.1 %all-to-all-done.5 = f32[4,1,256,640]{2,3,1,0:T(8,128)} async-done(((f32[4,1,256,640]{2,3,1,0:T(8,128)}), f32[4,1,256,640]{2,3,1,0:T(8,128)}, u32[]{:S(2)}, u32[]{:S(2)}) %all-to-all-start.5) | async-done | bytes 2621472 | tf_op jit(solution)/shard_map/all_to_all | solution.py:43
  419.8 16.4 %concatenate.52 = bf16[960,4481]{1,0:T(8,128)(2,1)} concatenate(bf16[960,1]{1,0:T(8,128)(2,1)} %convert_element_type.296, bf16[960,960]{1,0:T(8,128)(2,1)S(1)} %convolution_convert_fusion.1, bf16[960,320]{1,0:T(8,128)(2,1)} %copy.220, bf16[960,320]{1,0:T(8,128)(2,1)} %copy.221, bf16[960,960]{1,0:T(8,128)(2,1)} %convolution_convert_fusion, ...), dimensions={1} | concatenate | bytes 17207040 | tf_op jit(solution)/shard_map/concatenate | solution.py:49
  441.0 88.6 %reduce-scatter.2.cloned.1.call-done = bf16[120,4481]{1,0:T(8,128)(2,1)} async-done(((bf16[960,4481]{1,0:T(8,128)(2,1)}), bf16[120,4481]{1,0:T(8,128)(2,1)}) %reduce-scatter.2.cloned.1.call-update) | async-done | bytes 1075456 | tf_op jit(solution)/shard_map/reduce_scatter | solution.py:50
  538.1 9.2 %all-to-all-done.8 = bf16[4,120,640]{2,1,0:T(8,128)(2,1)} async-done(((bf16[4,120,640]{2,1,0:T(8,128)(2,1)}), bf16[4,120,640]{2,1,0:T(8,128)(2,1)}, u32[]{:S(2)}, u32[]{:S(2)}) %all-to-all-start.8) | async-done | bytes 614432 | tf_op jit(solution)/shard_map/all_to_all | solution.py:22
  555.5 7.4 %all-to-all-done.7 = bf16[4,120,640]{2,1,0:T(8,128)(2,1)S(1)} async-done(((bf16[4,120,640]{2,1,0:T(8,128)(2,1)}), bf16[4,120,640]{2,1,0:T(8,128)(2,1)S(1)}, u32[]{:S(2)}, u32[]{:S(2)}) %all-to-all-start.7) | async-done | bytes 614432 | tf_op jit(solution)/shard_map/all_to_all | solution.py:22
  569.1 20.6 %all-reduce.2 = bf16[960]{0:T(1024)(128)(2,1)S(1)} all-reduce(bf16[960]{0:T(1024)(128)(2,1)S(1)} %get-tuple-element.79), channel_id=2, replica_groups=mesh['fsdp'=8,'ctx'=4,'tp'=4] {'fsdp'}, use_global_device_ids=true, to_apply=%region_23.24.clone | all-reduce | flops 960 | bytes 3840
  590.7 34.6 %all-reduce.3 = (bf16[120]{0:T(256)(128)(2,1)S(1)}, bf16[120]{0:T(256)(128)(2,1)S(1)}) all-reduce(bf16[120]{0:T(256)(128)(2,1)S(1)} %dynamic-slice.3, bf16[120]{0:T(256)(128)(2,1)S(1)} %slice_reduce_fusion), channel_id=1, replica_groups=mesh['fsdp'=8,'ctx'=4,'tp'=4] {'ctx','tp'}, use_global_device_ids=true, to_apply=%region_24.25 | all-reduce | flops 240 | bytes 960 | tf_op jit(solution)/shard_map/psum | solution.py:359
  630.9 64.3 %all-reduce.8.cloned.1.call-done = (bf16[120,320]{1,0:T(8,128)(2,1)}, bf16[120,320]{1,0:T(8,128)(2,1)}, bf16[120,960]{1,0:T(8,128)(2,1)}, bf16[120,960]{1,0:T(8,128)(2,1)}) async-done(((bf16[120,320]{1,0:T(8,128)(2,1)}, bf16[120,320]{1,0:T(8,128)(2,1)}, bf16[120,960]{1,0:T(8,128)(2,1)}, bf16[120,960]{1,0:T(8,128)(2,1)}), (bf16[120,320]{1,0:T(8,128)(2,1)}, bf16[120,320]{1,0:T(8,128)(2,1)}, ...) | async-done | bytes 614416 | tf_op jit(solution)/shard_map/psum | solution.py:362
  (279 shorter events, 226.9 us)
Async XLA Ops:
  7.2 137.2 %all-gather.8.cloned.1.call-start = ((), (), s32[]{:S(2)}) async-start(), calls=%async_computation.10 | async-start | bytes 2211840 | tf_op jit(solution)/shard_map/all_gather | solution.py:144
  7.9 155.0 %all-gather.10.cloned.1.call-start = ((), (), s32[]{:S(2)}) async-start(), calls=%async_computation.11 | async-start | bytes 2211840 | tf_op jit(solution)/shard_map/all_gather | solution.py:147
  8.7 194.3 %all-gather.14.cloned.1.call-start = ((), (), s32[]{:S(2)}) async-start(), calls=%async_computation.13 | async-start | bytes 1382400 | tf_op jit(solution)/shard_map/all_gather | solution.py:149
  99.5 32.7 %all-to-all-start = ((bf16[4,1,256,640]{2,3,1,0:T(8,128)(2,1)}), bf16[4,1,256,640]{2,3,1,0:T(8,128)(2,1)S(1)}, u32[]{:S(2)}, u32[]{:S(2)}) async-start(bf16[4,1,256,640]{2,3,1,0:T(8,128)(2,1)} %broadcast_in_dim.38), calls=%async_computation | async-start | bytes 2621440 | tf_op jit(solution)/shard_map/all_to_all | solution.py:22
  104.2 104.1 %all-gather.12.cloned.1.call-start = ((), (), s32[]{:S(2)}) async-start(), calls=%async_computation.12 | async-start | bytes 1382400 | tf_op jit(solution)/shard_map/all_gather | solution.py:148
  105.6 42.8 %copy-start.30 = (pred[256,1024]{0,1:T(8,128)(4,1)}, pred[256,1024]{0,1:T(8,128)(4,1)S(1)}, u32[]{:S(2)}) copy-start(pred[256,1024]{0,1:T(8,128)(4,1)S(1)} %iota_compare_fusion) | copy-start | bytes 786436
  134.6 33.0 %all-to-all-start.3 = ((bf16[4,1,256,960]{2,3,1,0:T(8,128)(2,1)}), bf16[4,1,256,960]{2,3,1,0:T(8,128)(2,1)}, u32[]{:S(2)}, u32[]{:S(2)}) async-start(bf16[4,1,256,960]{2,3,1,0:T(8,128)(2,1)} %broadcast_in_dim.78), calls=%async_computation.3 | async-start | bytes 3932160 | tf_op jit(solution)/shard_map/all_to_all | solution.py:22
  153.0 7.4 %copy-start.3 = (f32[1,3,256,1024]{2,3,1,0:T(8,128)}, f32[1,3,256,1024]{2,3,1,0:T(8,128)S(1)}, u32[]{:S(2)}) copy-start(f32[1,3,256,1024]{2,3,1,0:T(8,128)S(1)} %get-tuple-element.122) | copy-start | bytes 9437188
  153.7 7.9 %copy-start.8 = (f32[1,3,256,1024]{2,3,1,0:T(8,128)}, f32[1,3,256,1024]{2,3,1,0:T(8,128)S(1)}, u32[]{:S(2)}) copy-start(f32[1,3,256,1024]{2,3,1,0:T(8,128)S(1)} %get-tuple-element.124) | copy-start | bytes 9437188
  170.0 28.2 %all-to-all-start.1 = ((bf16[4,1,256,960]{2,3,1,0:T(8,128)(2,1)}), bf16[4,1,256,960]{2,3,1,0:T(8,128)(2,1)}, u32[]{:S(2)}, u32[]{:S(2)}) async-start(bf16[4,1,256,960]{2,3,1,0:T(8,128)(2,1)} %broadcast_in_dim.77), calls=%async_computation.1 | async-start | bytes 3932160 | tf_op jit(solution)/shard_map/all_to_all | solution.py:22
  174.8 44.8 %all-gather.16.cloned.1.call-start = ((), (), s32[]{:S(2)}) async-start(), calls=%async_computation.14 | async-start | bytes 1382400 | tf_op jit(solution)/shard_map/all_gather | solution.py:150
  219.6 8.9 %copy-start.53 = (bf16[960,640]{1,0:T(8,128)(2,1)S(1)}, bf16[960,640]{1,0:T(8,128)(2,1)}, u32[]{:S(2)}) copy-start(bf16[960,640]{1,0:T(8,128)(2,1)} %all-gather.16.cloned.1.call-done) | copy-start | bytes 3686404
  239.2 24.8 %all-to-all-start.2 = ((bf16[4,1,256,960]{2,3,1,0:T(8,128)(2,1)}), bf16[4,1,256,960]{2,3,1,0:T(8,128)(2,1)}, u32[]{:S(2)}, u32[]{:S(2)}) async-start(bf16[4,1,256,960]{2,3,1,0:T(8,128)(2,1)} %copy.199), calls=%async_computation.2 | async-start | bytes 3932160 | tf_op jit(solution)/shard_map/all_to_all | solution.py:37
  264.0 44.9 %all-to-all-start.4 = ((f32[4,1,256,960]{2,3,1,0:T(8,128)}), f32[4,1,256,960]{2,3,1,0:T(8,128)}, u32[]{:S(2)}, u32[]{:S(2)}) async-start(f32[4,1,256,960]{2,3,1,0:T(8,128)} %copy.201), calls=%async_computation.4 | async-start | bytes 7864320 | tf_op jit(solution)/shard_map/all_to_all | solution.py:43
  351.0 11.8 %copy-start.20 = (bf16[3,256,1024]{1,2,0:T(8,128)(2,1)}, bf16[3,256,1024]{1,2,0:T(8,128)(2,1)S(1)}, u32[]{:S(2)}) copy-start(bf16[3,256,1024]{1,2,0:T(8,128)(2,1)S(1)} %fusion.34) | copy-start | bytes 4718596
  352.7 8.7 %copy-start.15 = (bf16[3,256,1024]{1,2,0:T(8,128)(2,1)}, bf16[3,256,1024]{1,2,0:T(8,128)(2,1)S(1)}, u32[]{:S(2)}) copy-start(bf16[3,256,1024]{1,2,0:T(8,128)(2,1)S(1)} %fusion.33) | copy-start | bytes 4718596
  368.0 7.5 %copy-start.18 = (bf16[3,256,1024]{1,2,0:T(8,128)(2,1)S(1)}, bf16[3,256,1024]{1,2,0:T(8,128)(2,1)}, u32[]{:S(2)}) copy-start(bf16[3,256,1024]{1,2,0:T(8,128)(2,1)} %copy-done.17) | copy-start | bytes 4718596
  368.0 37.6 %all-to-all-start.5 = ((f32[4,1,256,640]{2,3,1,0:T(8,128)}), f32[4,1,256,640]{2,3,1,0:T(8,128)}, u32[]{:S(2)}, u32[]{:S(2)}) async-start(f32[4,1,256,640]{2,3,1,0:T(8,128)} %pad_maximum_fusion), calls=%async_computation.5 | async-start | bytes 5242880 | tf_op jit(solution)/shard_map/all_to_all | solution.py:43
  372.8 156.8 %reduce-scatter.2.cloned.1.call-start = ((), (), s32[]{:S(2)}) async-start(), calls=%async_computation.15 | async-start | bytes 9953280 | tf_op jit(solution)/shard_map/reduce_scatter | solution.py:50
  439.6 96.4 %copy-start.37 = (f32[256,640]{0,1:T(8,128)S(1)}, f32[256,640]{0,1:T(8,128)}, u32[]{:S(2)}) copy-start(f32[256,640]{0,1:T(8,128)} %reduce_sum.213) | copy-start | bytes 1966084
  531.8 15.5 %all-to-all-start.8 = ((bf16[4,120,640]{2,1,0:T(8,128)(2,1)}), bf16[4,120,640]{2,1,0:T(8,128)(2,1)}, u32[]{:S(2)}, u32[]{:S(2)}) async-start(bf16[4,120,640]{2,1,0:T(8,128)(2,1)} %broadcast_in_dim.81), calls=%async_computation.9 | async-start | bytes 1228800 | tf_op jit(solution)/shard_map/all_to_all | solution.py:22
  548.2 14.7 %all-to-all-start.7 = ((bf16[4,120,640]{2,1,0:T(8,128)(2,1)}), bf16[4,120,640]{2,1,0:T(8,128)(2,1)S(1)}, u32[]{:S(2)}, u32[]{:S(2)}) async-start(bf16[4,120,640]{2,1,0:T(8,128)(2,1)} %broadcast_in_dim.80), calls=%async_computation.8 | async-start | bytes 1228800 | tf_op jit(solution)/shard_map/all_to_all | solution.py:22
  551.7 143.6 %all-reduce.8.cloned.1.call-start = ((), (), s32[]{:S(2)}) async-start(), calls=%async_computation.16 | async-start | bytes 1351680 | tf_op jit(solution)/shard_map/psum | solution.py:362
  563.8 65.2 %all-to-all-start.6 = ((bf16[4,120,640]{2,1,0:T(8,128)(2,1)}), bf16[4,120,640]{2,1,0:T(8,128)(2,1)}, u32[]{:S(2)}, u32[]{:S(2)}) async-start(bf16[4,120,640]{2,1,0:T(8,128)(2,1)} %broadcast_in_dim.79), calls=%async_computation.7 | async-start | bytes 1228800 | tf_op jit(solution)/shard_map/all_to_all | solution.py:22
  (48 other events, 146.5 us)
Sparse Core Ops, SparseCore 0:
  9.6 43.5 all-gather.7
  54.9 41.9 all-gather.9
  98.5 40.3 all-gather.13
  140.5 39.3 all-gather.11
  181.3 38.2 all-gather.15
  436.3 93.1 reduce-scatter.1
  555.8 139.4 all-reduce.7
where the time goes:
time: 716 us; the launch traced here: 709 us
  waiting for transfers between devices  270 us (38%)
  blocking collectives  136 us (19%)
  local copies, waits for them, and re-layouts  102 us (14%)
  matrix products  102 us (14%)
  starting transfers between devices  41.3 us (6%)
  other arithmetic  41.3 us (6%)
  between operations  17.3 us (2%)
    reduce_scatter x1, waiting for transfers between devices, sent_together(): lax.psum_scatter(both, axis, scatter_dimension=dim, tiled=True)  88.6 us
    psum x1, waiting for transfers between devices, shards(): lax.psum(share_key.astype(jnp.bfloat16), ('ctx', 'tp')).astype(jnp.float32)  64.3 us
    all_to_all x6, waiting for transfers between devices, from_everyone(): return lax.all_to_all(copies, axis, split_axis=0, concat_axis=0, tiled=True)  60.2 us
    all_to_all x2, waiting for transfers between devices, sum_at_owner(): lax.all_to_all(tiles, axis, split_axis=0, concat_axis=0, tiled=True)  44.8 us
    unnamed x2, blocking collectives  38.9 us
    psum x1, blocking collectives, shards(): lax.psum(share_gain_one.astype(jnp.bfloat16), ('ctx', 'tp'))  34.6 us
    all_gather x1, blocking collectives, shards(): lax.all_gather(w_key, 'fsdp', axis=0, tiled=True)  31.9 us
    all_gather x1, blocking collectives, shards(): lax.all_gather(w_value, 'fsdp', axis=0, tiled=True)  31 us
  transfers between devices with their start and end apart: 16, of which 10 were waited for; matrix products, arithmetic and copies ran while one was open for 17% of the time, Pallas kernels for 0%

commit v1 on v0

--- a/solution.py
+++ b/solution.py
@@ -356,7 +356,9 @@
         over_copies(share_down.astype(jnp.bfloat16), "ctx").astype(jnp.float32),
     )
     share_gain_one, share_gain_two, share_query, share_key, share_value, share_out = (
-        lax.psum(share_gain_one.astype(jnp.bfloat16), ("ctx", "tp")).astype(jnp.float32),
+        jnp.sum(lax.all_gather(share_gain_one.astype(jnp.bfloat16), ("ctx", "tp")), axis=0).astype(
+            jnp.float32
+        ),
         lax.psum(share_gain_two.astype(jnp.bfloat16), ("ctx", "tp")).astype(jnp.float32),
         lax.psum(share_query.astype(jnp.bfloat16), ("ctx", "tp")).astype(jnp.float32),
         lax.psum(share_key.astype(jnp.bfloat16), ("ctx", "tp")).astype(jnp.float32),

time: 716 us -> 716 us (level)
    unnamed x2 -> x3, blocking collectives: 38.9 us -> 74 us
    psum x1 -> x0, blocking collectives: 34.6 us -> none  [shards(): lax.psum(share_gain_one.astype(jnp.bfloat16), ('ctx', 'tp'))]
    unnamed x124 -> x129, local copies, waits for them, and re-layouts: 24.1 us -> 24.8 us
where the time goes in v1:
time: 716 us; the launch traced here: 709 us
  waiting for transfers between devices  268 us (37%)
  blocking collectives  137 us (19%)
  local copies, waits for them, and re-layouts  102 us (14%)
  matrix products  102 us (14%)
  starting transfers between devices  41.3 us (6%)
  other arithmetic  41.3 us (6%)
  between operations  17.9 us (2%)
    reduce_scatter x1, waiting for transfers between devices, sent_together(): lax.psum_scatter(both, axis, scatter_dimension=dim, tiled=True)  87.6 us
    unnamed x3, blocking collectives  74 us
    psum x1, waiting for transfers between devices, shards(): lax.psum(share_key.astype(jnp.bfloat16), ('ctx', 'tp')).astype(jnp.float32)  63.5 us
    all_to_all x6, waiting for transfers between devices, from_everyone(): return lax.all_to_all(copies, axis, split_axis=0, concat_axis=0, tiled=True)  60.2 us
    all_to_all x2, waiting for transfers between devices, sum_at_owner(): lax.all_to_all(tiles, axis, split_axis=0, concat_axis=0, tiled=True)  44.9 us
    all_gather x1, blocking collectives, shards(): lax.all_gather(w_key, 'fsdp', axis=0, tiled=True)  31.9 us
    all_gather x1, blocking collectives, shards(): lax.all_gather(w_value, 'fsdp', axis=0, tiled=True)  31 us
    all_to_all x6, starting transfers between devices, from_everyone(): return lax.all_to_all(copies, axis, split_axis=0, concat_axis=0, tiled=True)  26.5 us
  transfers between devices with their start and end apart: 16, of which 10 were waited for; matrix products, arithmetic and copies ran while one was open for 17% of the time, Pallas kernels for 0%

profile of v1, /device:TPU:0, one launch (start us, length us, event | category | flops | bytes accessed | tf_op | source)
XLA Modules:
  0.0 709.2 jit_solution(7344623231868554522)
XLA Ops:
  9.4 31.9 %all-gather.1 = bf16[8,120,320]{1,2,0:T(8,128)(2,1)S(1)} all-gather(bf16[1,120,320]{1,2,0:T(8,128)(2,1)} %bitcast.613), channel_id=1, replica_groups=mesh['fsdp'=8,'ctx'=4,'tp'=4] {'fsdp'}, dimensions={0}, use_global_device_ids=true | all-gather | bytes 691200 | tf_op jit(solution)/shard_map/all_gather | solution.py:145
  41.3 31.0 %all-gather.2 = bf16[8,120,320]{1,2,0:T(8,128)(2,1)S(1)} all-gather(bf16[1,120,320]{1,2,0:T(8,128)(2,1)} %bitcast.614), channel_id=1, replica_groups=mesh['fsdp'=8,'ctx'=4,'tp'=4] {'fsdp'}, dimensions={0}, use_global_device_ids=true | all-gather | bytes 691200 | tf_op jit(solution)/shard_map/all_gather | solution.py:146
  76.7 18.3 %all-reduce.6 = (bf16[960]{0:T(1024)(128)(2,1)S(1)}, bf16[960]{0:T(1024)(128)(2,1)S(1)}) all-reduce(bf16[960]{0:T(1024)(128)(2,1)S(1)} %dynamic-update-slice, bf16[960]{0:T(1024)(128)(2,1)S(1)} %dynamic-update-slice.1), channel_id=1, replica_groups=mesh['fsdp'=8,'ctx'=4,'tp'=4] {'fsdp'}, use_global_device_ids=true, to_apply=%add | all-reduce | flops 1920 | bytes 7680
  106.5 25.6 %all-to-all-done = bf16[4,1,256,640]{2,3,1,0:T(8,128)(2,1)S(1)} async-done(((bf16[4,1,256,640]{2,3,1,0:T(8,128)(2,1)}), bf16[4,1,256,640]{2,3,1,0:T(8,128)(2,1)S(1)}, u32[]{:S(2)}, u32[]{:S(2)}) %all-to-all-start) | async-done | bytes 1310752 | tf_op jit(solution)/shard_map/all_to_all | solution.py:22
  134.6 5.3 all-to-all-start.3
  170.0 4.8 all-to-all-start.1
  180.2 18.0 %all-to-all-done.1 = bf16[4,1,256,960]{2,3,1,0:T(8,128)(2,1)} async-done(((bf16[4,1,256,960]{2,3,1,0:T(8,128)(2,1)}), bf16[4,1,256,960]{2,3,1,0:T(8,128)(2,1)}, u32[]{:S(2)}, u32[]{:S(2)}) %all-to-all-start.1) | async-done | bytes 1966112 | tf_op jit(solution)/shard_map/all_to_all | solution.py:22
  203.0 5.3 fusion.133
  208.3 5.2 fusion.132
  213.5 6.0 all-gather.17.cloned.1.call-done
  219.5 7.8 %multiply_convert_fusion = (bf16[1024,640]{1,0:T(8,128)(2,1)}, bf16[1024,640]{1,0:T(8,128)(2,1)}, bf16[1024,640]{1,0:T(8,128)(2,1)S(1)}) fusion(f32[1024,640]{1,0:T(8,128)} %fusion.132, f32[1024,640]{1,0:T(8,128)} %fusion.133, bf16[1024,960]{0,1:T(8,128)(2,1)} %bitcast.599, bf16[960,640]{1,0:T(8,128)(2,1)} %all-gather.17.cloned.1.call-done), kind=kOutput, calls=%fused_computation.47 | convolution fusion | flops 1268776960 | bytes 12369920 | tf_op jit(solution)/shard_map/dot_general | solution.py:225
  250.9 5.5 reshape_reshape.11
  256.3 4.7 copy.201
  263.9 5.0 all-to-all-start.4
  268.9 4.8 convolution_convert_fusion.3
  282.1 26.7 %all-to-all-done.4 = f32[4,1,256,960]{2,3,1,0:T(8,128)} async-done(((f32[4,1,256,960]{2,3,1,0:T(8,128)}), f32[4,1,256,960]{2,3,1,0:T(8,128)}, u32[]{:S(2)}, u32[]{:S(2)}) %all-to-all-start.4) | async-done | bytes 3932192 | tf_op jit(solution)/shard_map/all_to_all | solution.py:43
  387.5 18.1 %all-to-all-done.5 = f32[4,1,256,640]{2,3,1,0:T(8,128)} async-done(((f32[4,1,256,640]{2,3,1,0:T(8,128)}), f32[4,1,256,640]{2,3,1,0:T(8,128)}, u32[]{:S(2)}, u32[]{:S(2)}) %all-to-all-start.5) | async-done | bytes 2621472 | tf_op jit(solution)/shard_map/all_to_all | solution.py:43
  419.8 16.3 %concatenate.52 = bf16[960,4481]{1,0:T(8,128)(2,1)} concatenate(bf16[960,1]{1,0:T(8,128)(2,1)} %convert_element_type.298, bf16[960,960]{1,0:T(8,128)(2,1)S(1)} %convolution_convert_fusion.1, bf16[960,320]{1,0:T(8,128)(2,1)} %copy.220, bf16[960,320]{1,0:T(8,128)(2,1)} %copy.221, bf16[960,960]{1,0:T(8,128)(2,1)} %convolution_convert_fusion, ...), dimensions={1} | concatenate | bytes 17207040 | tf_op jit(solution)/shard_map/concatenate | solution.py:49
  442.0 87.6 %reduce-scatter.2.cloned.1.call-done = bf16[120,4481]{1,0:T(8,128)(2,1)} async-done(((bf16[960,4481]{1,0:T(8,128)(2,1)}), bf16[120,4481]{1,0:T(8,128)(2,1)}) %reduce-scatter.2.cloned.1.call-update) | async-done | bytes 1075456 | tf_op jit(solution)/shard_map/reduce_scatter | solution.py:50
  538.1 9.2 %all-to-all-done.8 = bf16[4,120,640]{2,1,0:T(8,128)(2,1)} async-done(((bf16[4,120,640]{2,1,0:T(8,128)(2,1)}), bf16[4,120,640]{2,1,0:T(8,128)(2,1)}, u32[]{:S(2)}, u32[]{:S(2)}) %all-to-all-start.8) | async-done | bytes 614432 | tf_op jit(solution)/shard_map/all_to_all | solution.py:22
  555.5 7.4 %all-to-all-done.7 = bf16[4,120,640]{2,1,0:T(8,128)(2,1)S(1)} async-done(((bf16[4,120,640]{2,1,0:T(8,128)(2,1)}), bf16[4,120,640]{2,1,0:T(8,128)(2,1)S(1)}, u32[]{:S(2)}, u32[]{:S(2)}) %all-to-all-start.7) | async-done | bytes 614432 | tf_op jit(solution)/shard_map/all_to_all | solution.py:22
  569.1 20.6 %all-reduce.3 = bf16[960]{0:T(1024)(128)(2,1)S(1)} all-reduce(bf16[960]{0:T(1024)(128)(2,1)S(1)} %get-tuple-element.79), channel_id=3, replica_groups=mesh['fsdp'=8,'ctx'=4,'tp'=4] {'fsdp'}, use_global_device_ids=true, to_apply=%region_23.24.clone | all-reduce | flops 960 | bytes 3840
  590.8 35.1 %all-reduce.4 = (bf16[1920]{0:T(1024)(128)(2,1)S(1)}, bf16[120]{0:T(256)(128)(2,1)S(1)}) all-reduce(bf16[1920]{0:T(1024)(128)(2,1)S(1)} %dynamic-update-slice.2, bf16[120]{0:T(256)(128)(2,1)S(1)} %slice_reduce_fusion), channel_id=2, replica_groups=mesh['fsdp'=8,'ctx'=4,'tp'=4] {'ctx','tp'}, use_global_device_ids=true, to_apply=%add.2 | all-reduce | flops 2040 | bytes 8160
  631.7 63.5 %all-reduce.9.cloned.1.call-done = (bf16[120,320]{1,0:T(8,128)(2,1)}, bf16[120,320]{1,0:T(8,128)(2,1)}, bf16[120,960]{1,0:T(8,128)(2,1)}, bf16[120,960]{1,0:T(8,128)(2,1)}) async-done(((bf16[120,320]{1,0:T(8,128)(2,1)}, bf16[120,320]{1,0:T(8,128)(2,1)}, bf16[120,960]{1,0:T(8,128)(2,1)}, bf16[120,960]{1,0:T(8,128)(2,1)}), (bf16[120,320]{1,0:T(8,128)(2,1)}, bf16[120,320]{1,0:T(8,128)(2,1)}, ...) | async-done | bytes 614416 | tf_op jit(solution)/shard_map/psum | solution.py:364
  (286 shorter events, 227.6 us)
Async XLA Ops:
  7.2 137.2 %all-gather.9.cloned.1.call-start = ((), (), s32[]{:S(2)}) async-start(), calls=%async_computation.10 | async-start | bytes 2211840 | tf_op jit(solution)/shard_map/all_gather | solution.py:144
  7.9 155.0 %all-gather.11.cloned.1.call-start = ((), (), s32[]{:S(2)}) async-start(), calls=%async_computation.11 | async-start | bytes 2211840 | tf_op jit(solution)/shard_map/all_gather | solution.py:147
  8.7 194.3 %all-gather.15.cloned.1.call-start = ((), (), s32[]{:S(2)}) async-start(), calls=%async_computation.13 | async-start | bytes 1382400 | tf_op jit(solution)/shard_map/all_gather | solution.py:149
  99.5 32.7 %all-to-all-start = ((bf16[4,1,256,640]{2,3,1,0:T(8,128)(2,1)}), bf16[4,1,256,640]{2,3,1,0:T(8,128)(2,1)S(1)}, u32[]{:S(2)}, u32[]{:S(2)}) async-start(bf16[4,1,256,640]{2,3,1,0:T(8,128)(2,1)} %broadcast_in_dim.38), calls=%async_computation | async-start | bytes 2621440 | tf_op jit(solution)/shard_map/all_to_all | solution.py:22
  104.2 104.1 %all-gather.13.cloned.1.call-start = ((), (), s32[]{:S(2)}) async-start(), calls=%async_computation.12 | async-start | bytes 1382400 | tf_op jit(solution)/shard_map/all_gather | solution.py:148
  105.6 42.8 %copy-start.30 = (pred[256,1024]{0,1:T(8,128)(4,1)}, pred[256,1024]{0,1:T(8,128)(4,1)S(1)}, u32[]{:S(2)}) copy-start(pred[256,1024]{0,1:T(8,128)(4,1)S(1)} %iota_compare_fusion) | copy-start | bytes 786436
  134.6 33.0 %all-to-all-start.3 = ((bf16[4,1,256,960]{2,3,1,0:T(8,128)(2,1)}), bf16[4,1,256,960]{2,3,1,0:T(8,128)(2,1)}, u32[]{:S(2)}, u32[]{:S(2)}) async-start(bf16[4,1,256,960]{2,3,1,0:T(8,128)(2,1)} %broadcast_in_dim.78), calls=%async_computation.3 | async-start | bytes 3932160 | tf_op jit(solution)/shard_map/all_to_all | solution.py:22
  153.0 7.4 %copy-start.3 = (f32[1,3,256,1024]{2,3,1,0:T(8,128)}, f32[1,3,256,1024]{2,3,1,0:T(8,128)S(1)}, u32[]{:S(2)}) copy-start(f32[1,3,256,1024]{2,3,1,0:T(8,128)S(1)} %get-tuple-element.122) | copy-start | bytes 9437188
  153.7 7.9 %copy-start.8 = (f32[1,3,256,1024]{2,3,1,0:T(8,128)}, f32[1,3,256,1024]{2,3,1,0:T(8,128)S(1)}, u32[]{:S(2)}) copy-start(f32[1,3,256,1024]{2,3,1,0:T(8,128)S(1)} %get-tuple-element.124) | copy-start | bytes 9437188
  170.0 28.2 %all-to-all-start.1 = ((bf16[4,1,256,960]{2,3,1,0:T(8,128)(2,1)}), bf16[4,1,256,960]{2,3,1,0:T(8,128)(2,1)}, u32[]{:S(2)}, u32[]{:S(2)}) async-start(bf16[4,1,256,960]{2,3,1,0:T(8,128)(2,1)} %broadcast_in_dim.77), calls=%async_computation.1 | async-start | bytes 3932160 | tf_op jit(solution)/shard_map/all_to_all | solution.py:22
  174.8 44.8 %all-gather.17.cloned.1.call-start = ((), (), s32[]{:S(2)}) async-start(), calls=%async_computation.14 | async-start | bytes 1382400 | tf_op jit(solution)/shard_map/all_gather | solution.py:150
  219.5 8.9 %copy-start.53 = (bf16[960,640]{1,0:T(8,128)(2,1)S(1)}, bf16[960,640]{1,0:T(8,128)(2,1)}, u32[]{:S(2)}) copy-start(bf16[960,640]{1,0:T(8,128)(2,1)} %all-gather.17.cloned.1.call-done) | copy-start | bytes 3686404
  239.2 24.8 %all-to-all-start.2 = ((bf16[4,1,256,960]{2,3,1,0:T(8,128)(2,1)}), bf16[4,1,256,960]{2,3,1,0:T(8,128)(2,1)}, u32[]{:S(2)}, u32[]{:S(2)}) async-start(bf16[4,1,256,960]{2,3,1,0:T(8,128)(2,1)} %copy.199), calls=%async_computation.2 | async-start | bytes 3932160 | tf_op jit(solution)/shard_map/all_to_all | solution.py:37
  263.9 44.9 %all-to-all-start.4 = ((f32[4,1,256,960]{2,3,1,0:T(8,128)}), f32[4,1,256,960]{2,3,1,0:T(8,128)}, u32[]{:S(2)}, u32[]{:S(2)}) async-start(f32[4,1,256,960]{2,3,1,0:T(8,128)} %copy.201), calls=%async_computation.4 | async-start | bytes 7864320 | tf_op jit(solution)/shard_map/all_to_all | solution.py:43
  350.9 11.8 %copy-start.20 = (bf16[3,256,1024]{1,2,0:T(8,128)(2,1)}, bf16[3,256,1024]{1,2,0:T(8,128)(2,1)S(1)}, u32[]{:S(2)}) copy-start(bf16[3,256,1024]{1,2,0:T(8,128)(2,1)S(1)} %fusion.34) | copy-start | bytes 4718596
  352.7 8.7 %copy-start.15 = (bf16[3,256,1024]{1,2,0:T(8,128)(2,1)}, bf16[3,256,1024]{1,2,0:T(8,128)(2,1)S(1)}, u32[]{:S(2)}) copy-start(bf16[3,256,1024]{1,2,0:T(8,128)(2,1)S(1)} %fusion.33) | copy-start | bytes 4718596
  368.0 7.5 %copy-start.18 = (bf16[3,256,1024]{1,2,0:T(8,128)(2,1)S(1)}, bf16[3,256,1024]{1,2,0:T(8,128)(2,1)}, u32[]{:S(2)}) copy-start(bf16[3,256,1024]{1,2,0:T(8,128)(2,1)} %copy-done.17) | copy-start | bytes 4718596
  368.0 37.6 %all-to-all-start.5 = ((f32[4,1,256,640]{2,3,1,0:T(8,128)}), f32[4,1,256,640]{2,3,1,0:T(8,128)}, u32[]{:S(2)}, u32[]{:S(2)}) async-start(f32[4,1,256,640]{2,3,1,0:T(8,128)} %pad_maximum_fusion), calls=%async_computation.5 | async-start | bytes 5242880 | tf_op jit(solution)/shard_map/all_to_all | solution.py:43
  372.7 156.8 %reduce-scatter.2.cloned.1.call-start = ((), (), s32[]{:S(2)}) async-start(), calls=%async_computation.15 | async-start | bytes 9953280 | tf_op jit(solution)/shard_map/reduce_scatter | solution.py:50
  440.5 95.4 %copy-start.37 = (f32[256,640]{0,1:T(8,128)S(1)}, f32[256,640]{0,1:T(8,128)}, u32[]{:S(2)}) copy-start(f32[256,640]{0,1:T(8,128)} %reduce_sum.225) | copy-start | bytes 1966084
  531.8 15.5 %all-to-all-start.8 = ((bf16[4,120,640]{2,1,0:T(8,128)(2,1)}), bf16[4,120,640]{2,1,0:T(8,128)(2,1)}, u32[]{:S(2)}, u32[]{:S(2)}) async-start(bf16[4,120,640]{2,1,0:T(8,128)(2,1)} %broadcast_in_dim.81), calls=%async_computation.9 | async-start | bytes 1228800 | tf_op jit(solution)/shard_map/all_to_all | solution.py:22
  548.1 14.7 %all-to-all-start.7 = ((bf16[4,120,640]{2,1,0:T(8,128)(2,1)}), bf16[4,120,640]{2,1,0:T(8,128)(2,1)S(1)}, u32[]{:S(2)}, u32[]{:S(2)}) async-start(bf16[4,120,640]{2,1,0:T(8,128)(2,1)} %broadcast_in_dim.80), calls=%async_computation.8 | async-start | bytes 1228800 | tf_op jit(solution)/shard_map/all_to_all | solution.py:22
  551.6 143.6 %all-reduce.9.cloned.1.call-start = ((), (), s32[]{:S(2)}) async-start(), calls=%async_computation.16 | async-start | bytes 1351680 | tf_op jit(solution)/shard_map/psum | solution.py:364
  563.8 66.1 %all-to-all-start.6 = ((bf16[4,120,640]{2,1,0:T(8,128)(2,1)}), bf16[4,120,640]{2,1,0:T(8,128)(2,1)}, u32[]{:S(2)}, u32[]{:S(2)}) async-start(bf16[4,120,640]{2,1,0:T(8,128)(2,1)} %broadcast_in_dim.79), calls=%async_computation.7 | async-start | bytes 1228800 | tf_op jit(solution)/shard_map/all_to_all | solution.py:22
  (49 other events, 148.2 us)
Sparse Core Ops, SparseCore 0:
  9.6 43.5 all-gather.8
  54.9 41.9 all-gather.10
  98.5 40.3 all-gather.14
  140.5 39.3 all-gather.12
  181.3 38.1 all-gather.16
  436.3 93.1 reduce-scatter.1
  555.7 139.4 all-reduce.8
